TPU v7x, 32 devices: a whole 2x2x4 slice. The times are simulated.
32 devices in a mesh: dp: 4 (over z), lat: 4 (over y, core), lon: 2 (over x).
Axes of the slice: x: 2, y: 2, z: 4, core: 2. Of those that a mesh axis runs over, the one named last changes fastest.
Arguments:
- projected: bfloat16 [4, 4, 32, 16, 4608], P('dp', None, 'lat', 'lon'), may hold values from -52 to 52
- targets: bfloat16 [4, 4, 32, 16, 160], P('dp', None, 'lat', 'lon'), may hold values from -6 to 6
- valid_cells: int32 [32, 16], P('lat', 'lon'), may hold values 0 or 1
- w_out: bfloat16 [1536, 1536], P('dp'), may hold values from -0.15625 to 0.15625
- unpatch_matrix: bfloat16 [1536, 160], P('dp'), may hold values from -0.15625 to 0.15625
- norm_gain: bfloat16 [1536], P('dp'), may hold values from 0.099609375 to 1.8984375
- var_weight: float32 [5], replicated, may hold values from 0.3 to 3
Outputs:
- grad_context: bfloat16 [4, 4, 32, 16, 1536], P('dp', None, 'lat', 'lon')
- grad_recovery: float32 [1536, 160], P('dp')
- sample_penalty: float32 [4], P('dp')
All inputs are finite; a program needn't handle non-finite values. No bound on the sum of `valid_cells` on one device may be relied on, other than what follows from the above.
Results may differ from a plain program's by a relative error of at most 0.011.
Values may be sent and summed in bfloat16 or wider, within the bound.
No kernel may reach another device: no remote copies, remote signals or barrier semaphores. Data moves between devices by JAX's collectives and lax.ppermute only.
A program may use at most 64 MiB of HBM per device.

v0:
```python
import math
import jax
import jax.numpy as jnp
from jax import lax
from jax.sharding import PartitionSpec as P

HEADS = 48
HDIM = 32
WLEV = 2


def from_behind(array, axis, by):
    length = lax.axis_size(axis)
    return lax.ppermute(array, axis, [(i, (i + by) % length) for i in range(length)])


def shards(projected, targets, valid_cells, w_out, unpatch_matrix, norm_gain, var_weight):
    tile_side = projected.shape[2]
    half_side = tile_side // 2
    levels = projected.shape[1]
    model_width = w_out.shape[1]
    predicted_span = unpatch_matrix.shape[1]
    lat_total = tile_side * lax.axis_size("lat")
    lon_total = tile_side * lax.axis_size("lon")
    lat_place = lax.axis_index("lat")
    moved = from_behind(
        (projected[:, :, :, :half_side], targets[:, :, :, :half_side], valid_cells[:, :half_side]),
        "lon",
        -1,
    )
    strip_proj = jnp.concatenate([projected[:, :, :, half_side:], moved[0]], axis=3)
    strip_goal = jnp.concatenate([targets[:, :, :, half_side:], moved[1]], axis=3)
    strip_valid = jnp.concatenate([valid_cells[:, half_side:], moved[2]], axis=1)
    moved_rows = from_behind(
        (strip_proj[:, :, :half_side], strip_goal[:, :, :half_side], strip_valid[:half_side]),
        "lat",
        -1,
    )
    local_proj = jnp.concatenate([strip_proj[:, :, half_side:], moved_rows[0]], axis=2)
    shard_reference = jnp.concatenate([strip_goal[:, :, half_side:], moved_rows[1]], axis=2)
    local_valid = jnp.concatenate([strip_valid[half_side:], moved_rows[2]], axis=0).astype(
        jnp.float32
    )
    win_count = levels // WLEV
    tokw = WLEV * tile_side * tile_side
    windows = local_proj.reshape(win_count, tokw, 3 * model_width)
    rows_here = lat_place * tile_side + jnp.arange(tile_side)
    region_rows = (rows_here >= lat_total - half_side).astype(jnp.int32)
    region = jnp.broadcast_to(region_rows[None, :, None], (WLEV, tile_side, tile_side)).reshape(-1)
    allowed = region[:, None] == region[None, :]
    queries = windows[..., :model_width].reshape(win_count, tokw, HEADS, -1)
    key_heads = windows[..., model_width : 2 * model_width].reshape(win_count, tokw, HEADS, -1)
    value_heads = windows[..., 2 * model_width :].reshape(win_count, tokw, HEADS, -1)
    scores = jnp.einsum("wqhd,wkhd->whqk", queries, key_heads, preferred_element_type=jnp.float32)
    scores = scores * (1.0 / math.sqrt(HDIM))
    scores = jnp.where(allowed[None, None], scores, -1e30)
    row_peak = jnp.max(scores, axis=-1, keepdims=True)
    lifted = jnp.exp(scores - row_peak)
    attn = (lifted / jnp.sum(lifted, axis=-1, keepdims=True)).astype(jnp.bfloat16)
    context = jnp.einsum("whqk,wkhd->wqhd", attn, value_heads, preferred_element_type=jnp.float32)
    context = context.astype(jnp.bfloat16).reshape(win_count * tokw, model_width)
    element_total = win_count * tokw
    out_all, unprojected_pieces, gain_all = (
        lax.all_gather(w_out, "dp", axis=0, tiled=True),
        lax.all_gather(unpatch_matrix, "dp", axis=0, tiled=True),
        lax.all_gather(norm_gain, "dp", axis=0, tiled=True),
    )
    mixed_rows = jnp.dot(context, out_all, preferred_element_type=jnp.float32)
    centre = jnp.mean(mixed_rows, axis=-1, keepdims=True)
    spread = jnp.mean((mixed_rows - centre) ** 2, axis=-1, keepdims=True)
    inv_spread = lax.rsqrt(spread + 1e-05)
    normed = (mixed_rows - centre) * inv_spread
    gain_f = gain_all.astype(jnp.float32)
    latent_activation = (normed * gain_f).astype(jnp.bfloat16)
    prediction_field = jnp.dot(
        latent_activation, unprojected_pieces, preferred_element_type=jnp.float32
    )
    prediction_misfit = prediction_field - shard_reference.reshape(
        element_total, predicted_span
    ).astype(jnp.float32)
    all_rows = jnp.arange(lat_total).astype(jnp.float32)
    cosine_mean = jnp.mean(jnp.cos(math.pi * ((all_rows + 0.5) / lat_total - 0.5)))
    initial_rows = ((rows_here + half_side) % lat_total).astype(jnp.float32)
    lat_here = jnp.cos(math.pi * ((initial_rows + 0.5) / lat_total - 0.5)) / cosine_mean
    element_factor = jnp.broadcast_to(
        lat_here[None, :, None] * local_valid[None], (levels, tile_side, tile_side)
    ).reshape(element_total, 1)
    variable_factor = jnp.repeat(var_weight, predicted_span // var_weight.shape[0])[None, :]
    shard_penalty = jnp.sum(
        element_factor * variable_factor * prediction_misfit * prediction_misfit
    ) / (levels * lat_total * lon_total * (predicted_span // var_weight.shape[0]))
    prediction_gradient = (2.0 * element_factor * variable_factor * prediction_misfit).astype(
        jnp.bfloat16
    )
    grad_shard = lax.psum_scatter(
        jnp.einsum(
            "td,to->do", latent_activation, prediction_gradient, preferred_element_type=jnp.float32
        ).astype(jnp.bfloat16),
        "dp",
        scatter_dimension=0,
        tiled=True,
    ).astype(jnp.float32)
    grad_sum, loss_sum = lax.psum((grad_shard, shard_penalty), ("lat", "lon"))
    grad_recovery = grad_sum / (levels * lat_total * lon_total)
    grad_hidden = jnp.einsum(
        "to,do->td", prediction_gradient, unprojected_pieces, preferred_element_type=jnp.float32
    )
    scaled_grad = grad_hidden * gain_f
    grad_mixed = inv_spread * (
        scaled_grad
        - jnp.mean(scaled_grad, axis=-1, keepdims=True)
        - normed * jnp.mean(scaled_grad * normed, axis=-1, keepdims=True)
    )
    grad_mixed = grad_mixed.astype(jnp.bfloat16)
    grad_context = jnp.einsum("tj,ij->ti", grad_mixed, out_all, preferred_element_type=jnp.float32)
    grad_context = grad_context.astype(jnp.bfloat16).reshape(
        1, levels, tile_side, tile_side, model_width
    )
    return (grad_context, grad_recovery, loss_sum.reshape(1))


def solution(mesh):
    placed = (
        P("dp", None, "lat", "lon", None),
        P("dp", None, "lat", "lon", None),
        P("lat", "lon"),
        P("dp", None),
        P("dp", None),
        P("dp"),
        P(),
    )
    return jax.shard_map(
        shards,
        mesh=mesh,
        in_specs=placed,
        out_specs=(P("dp", None, "lat", "lon", None), P("dp", None), P("dp")),
        check_vma=False,
    )
```

profile of v0, /device:TPU:0, one launch (start us, length us, event | category | flops | bytes accessed | tf_op | source)
XLA Modules:
  0.0 177.8 jit_solution(18439652945624654499)
XLA Ops:
  7.2 0.7 all-gather.3.cloned.1.call-update
  7.9 3.3 %fusion.33 = (bf16[1,4,8,4,4608]{4,3,2,1,0:T(4,128)(2,1)S(1)}, bf16[1,4,8,4,4608]{4,3,2,1,0:T(4,128)(2,1)S(1)}) fusion(bf16[1,4,8,8,4608]{4,3,2,1,0:T(8,128)(2,1)} %param.7), kind=kLoop, calls=%fused_computation.70 | loop fusion | bytes 4718592 | tf_op jit(solution)/shard_map/slice | solution.py:31
  11.5 3.0 %collective-permute-start = (bf16[1,4,8,4,4608]{4,2,3,1,0:T(8,128)(2,1)S(1)}, bf16[1,4,8,4,4608]{4,2,3,1,0:T(8,128)(2,1)}, u32[]{:S(2)}, u32[]{:S(2)}) collective-permute-start(bf16[1,4,8,4,4608]{4,2,3,1,0:T(8,128)(2,1)S(1)} %copy.37), channel_id=1, source_target_pairs={{0,1},{1,0},{2,3},{3,2},{4,5},{5,4},{6,7},{7,6},{8,9},{9,8},{10,11... | collective-permute-start | bytes 3538952 | tf_op jit(solution)/shard_map/ppermute | solution.py:14
  14.5 0.6 fusion.36
  15.5 1.7 collective-permute-start.4
  17.4 13.0 %all-gather = bf16[4,1,384]{2,1,0:T(2,128)(2,1)S(1)} all-gather(bf16[1,1,384]{2,1,0:T(2,128)(2,1)S(1)} %reshape.165), channel_id=1, replica_groups=mesh['dp'=4,'lat'=4,'lon'=2] {'dp'}, dimensions={0}, use_global_device_ids=true | all-gather | bytes 3840 | tf_op jit(solution)/shard_map/all_gather | solution.py:66
  30.4 0.6 cosine_reduce_fusion
  31.7 0.6 fusion.27
  32.3 21.7 %all_gather.11 = bf16[1536,160]{0,1:T(8,128)(2,1)S(1)} all-gather(bf16[384,160]{0,1:T(8,128)(2,1)S(1)} %copy-done.4), channel_id=1, replica_groups=mesh['dp'=4,'lat'=4,'lon'=2] {'dp'}, dimensions={0}, use_global_device_ids=true | all-gather | bytes 614400 | tf_op jit(solution)/shard_map/all_gather | solution.py:65
  54.0 0.7 broadcast_compare_fusion
  54.7 1.9 %copy.27 = bf16[1,4,8,4,4608]{4,3,2,1,0:T(4,128)(2,1)S(1)} copy(bf16[1,4,8,4,4608]{4,2,3,1,0:T(8,128)(2,1)} %collective-permute-done) | data formatting | bytes 2359296 | tf_op jit(solution)/shard_map/ppermute | solution.py:14
  56.6 2.2 %fusion.8 = (bf16[1,4,4,8,4608]{4,3,2,1,0:T(8,128)(2,1)S(1)}, bf16[1,4,4,8,4608]{4,3,2,1,0:T(8,128)(2,1)}) fusion(bf16[1,4,8,4,4608]{4,3,2,1,0:T(4,128)(2,1)S(1)} %get-tuple-element.12, bf16[1,4,8,4,4608]{4,3,2,1,0:T(4,128)(2,1)S(1)} %copy.27), kind=kLoop, calls=%fused_computation.22 | loop fusion | flops 4718592 | bytes 4718592 | tf_op jit(solution)/shard_map/concatenate | solution.py:31
  58.9 1.6 collective-permute-start.3
  60.6 12.2 %collective-permute-done.3 = s32[4,8]{1,0:T(4,128)S(1)} collective-permute-done((s32[4,8]{1,0:T(4,128)S(1)}, s32[4,8]{1,0:T(4,128)S(1)}, u32[]{:S(2)}, u32[]{:S(2)}) %collective-permute-start.3) | collective-permute-done | bytes 160 | tf_op jit(solution)/shard_map/ppermute | solution.py:14
  73.1 2.5 %collective-permute-start.5 = (bf16[1,4,4,8,160]{4,3,2,1,0:T(8,128)(2,1)S(1)}, bf16[1,4,4,8,160]{4,3,2,1,0:T(8,128)(2,1)S(1)}, u32[]{:S(2)}, u32[]{:S(2)}) collective-permute-start(bf16[1,4,4,8,160]{4,3,2,1,0:T(8,128)(2,1)S(1)} %get-tuple-element.17), channel_id=1, source_target_pairs={{0,6},{2,0},{4,2},{6,4},{1,7},{3,1},{5,3},{7,5},{8,14},{10,8},{12,... | collective-permute-start | bytes 122888 | tf_op jit(solution)/shard_map/ppermute | solution.py:14
  75.5 1.9 %collective-permute-done.5 = bf16[1,4,4,8,160]{4,3,2,1,0:T(8,128)(2,1)S(1)} collective-permute-done((bf16[1,4,4,8,160]{4,3,2,1,0:T(8,128)(2,1)S(1)}, bf16[1,4,4,8,160]{4,3,2,1,0:T(8,128)(2,1)S(1)}, u32[]{:S(2)}, u32[]{:S(2)}) %collective-permute-start.5) | collective-permute-done | bytes 40992 | tf_op jit(solution)/shard_map/ppermute | solution.py:14
  78.1 1.2 copy.29
  79.2 1.2 copy.30
  80.4 1.2 copy.28
  81.6 4.2 %fusion.37 = (f32[2,48,128]{2,1,0:T(8,128)S(1)}, f32[2,48,128,128]{2,3,1,0:T(8,128)}) fusion(pred[128,128]{0,1:T(8,128)(4,1)S(1)} %copy-done.5, bf16[2,128,48,32]{1,3,2,0:T(8,128)(2,1)S(1)} %bitcast.35, bf16[2,128,48,32]{1,3,2,0:T(8,128)(2,1)S(1)} %bitcast.36), kind=kOutput, calls=%fused_computation.74 | convolution fusion | flops 106954880 | bytes 7929856 | tf_op jit(solution)/shard_map/sub | solution.py:58
  85.7 3.7 %fusion.7 = bf16[2,128,48,32]{1,3,2,0:T(8,128)(2,1)S(1)} fusion(bf16[2,128,48,32]{1,3,2,0:T(8,128)(2,1)S(1)} %bitcast.37, f32[2,48,128,128]{2,3,1,0:T(8,128)} %get-tuple-element.25, f32[2,48,128]{2,1,0:T(8,128)S(1)} %get-tuple-element.24), kind=kOutput, calls=%fused_computation.21 | convolution fusion | flops 104202240 | bytes 7913472 | tf_op jit(solution)/shard_map/whqk,wkhd->wqhd/dot_general | solution.py:60
  89.5 0.8 copy.32
  90.3 19.3 %all-gather.3.cloned.1.call-done = bf16[1536,1536]{1,0:T(8,128)(2,1)} async-done(((bf16[384,1536]{1,0:T(8,128)(2,1)}), bf16[1536,1536]{1,0:T(8,128)(2,1)}) %all-gather.3.cloned.1.call-update) | async-done | bytes 4718608 | tf_op jit(solution)/shard_map/all_gather | solution.py:64
  109.6 3.8 %fusion.38 = (f32[256]{0:T(256)S(1)}, f32[256,1536]{1,0:T(8,128)S(1)}) fusion(bf16[1536,1536]{1,0:T(8,128)(2,1)} %all-gather.3.cloned.1.call-done, bf16[192,8,2,128]{3,2,1,0:T(2,128)(2,1)S(1)} %bitcast.38), kind=kOutput, calls=%fused_computation.75 | convolution fusion | flops 1208352512 | bytes 7078912 | tf_op jit(solution)/shard_map/dot_general | solution.py:68
  114.4 0.7 fusion.18
  115.5 1.2 copy.35
  117.3 0.6 fusion.31
  117.9 4.8 %convolution_convert_fusion = bf16[256,1536]{1,0:T(8,128)(2,1)} fusion(bf16[1536,1536]{1,0:T(8,128)(2,1)} %all-gather.3.cloned.1.call-done, f32[256,1536]{1,0:T(8,128)S(1)} %get-tuple-element.28, f32[256,1536]{1,0:T(8,128)S(1)} %get-tuple-element.27, f32[256]{0:T(256)S(1)} %get-tuple-element.29, f32[256]{0:T(256)S(1)} %get-tuple-element.30, ...), kind=kOutput, calls=%fused_computation.10 | convolution fusion | flops 1211105280 | bytes 8654848 | tf_op jit(solution)/shard_map/tj,ij->ti/dot_general | solution.py:115
  122.7 15.9 %reduce-scatter.4.cloned.1.call-done = bf16[384,160]{1,0:T(8,128)(2,1)} async-done(((bf16[1536,160]{1,0:T(8,128)(2,1)}), bf16[384,160]{1,0:T(8,128)(2,1)}) %reduce-scatter.4.cloned.1.call-update) | async-done | bytes 122896
  138.6 1.1 copy.36
  139.7 30.5 %all-reduce.2 = (f32[384,160]{0,1:T(8,128)S(1)}, f32[1]{0:T(128)}) all-reduce(bf16[384,160]{0,1:T(8,128)(2,1)S(1)} %copy.36, f32[1]{0:T(128)} %bitcast.7), channel_id=1, replica_groups=mesh['dp'=4,'lat'=4,'lon'=2] {'lat','lon'}, use_global_device_ids=true, to_apply=%region_8.9 | all-reduce | flops 61441 | bytes 368648 | tf_op jit(solution)/shard_map/psum | solution.py:103
  170.2 0.7 broadcast_multiply_fusion
  (58 shorter events, 3.3 us)
Async XLA Ops:
  7.2 102.4 %all-gather.3.cloned.1.call-start = ((), (), s32[]{:S(2)}) async-start(), calls=%async_computation.1 | async-start | bytes 5898240 | tf_op jit(solution)/shard_map/all_gather | solution.py:64
  7.9 130.7 %reduce-scatter.4.cloned.1.call-start = ((), (), s32[]{:S(2)}) async-start(), calls=%async_computation.2 | async-start | bytes 983040
  11.2 3.3 %copy-start.6 = (s32[8,8]{1,0:T(8,128)S(1)}, s32[8,8]{1,0:T(8,128)}, u32[]{:S(2)}) copy-start(s32[8,8]{1,0:T(8,128)} %param.9) | copy-start | bytes 772
  11.2 4.2 %copy-start.3 = (bf16[1,4,8,8,160]{4,3,2,1,0:T(8,128)(2,1)S(1)}, bf16[1,4,8,8,160]{4,3,2,1,0:T(8,128)(2,1)}, u32[]{:S(2)}) copy-start(bf16[1,4,8,8,160]{4,3,2,1,0:T(8,128)(2,1)} %param.8) | copy-start | bytes 245764
  11.3 6.1 %copy-start.7 = (bf16[384]{0:T(512)(128)(2,1)S(1)}, bf16[384]{0:T(512)(128)(2,1)}, u32[]{:S(2)}) copy-start(bf16[384]{0:T(512)(128)(2,1)} %param.12) | copy-start | bytes 2308
  11.3 21.0 %copy-start.4 = (bf16[384,160]{0,1:T(8,128)(2,1)S(1)}, bf16[384,160]{0,1:T(8,128)(2,1)}, u32[]{:S(2)}) copy-start(bf16[384,160]{0,1:T(8,128)(2,1)} %param.11) | copy-start | bytes 368644
  11.5 43.2 %collective-permute-start = (bf16[1,4,8,4,4608]{4,2,3,1,0:T(8,128)(2,1)S(1)}, bf16[1,4,8,4,4608]{4,2,3,1,0:T(8,128)(2,1)}, u32[]{:S(2)}, u32[]{:S(2)}) collective-permute-start(bf16[1,4,8,4,4608]{4,2,3,1,0:T(8,128)(2,1)S(1)} %copy.37), channel_id=1, source_target_pairs={{0,1},{1,0},{2,3},{3,2},{4,5},{5,4},{6,7},{7,6},{8,9},{9,8},{10,11... | collective-permute-start | bytes 3538952 | tf_op jit(solution)/shard_map/ppermute | solution.py:14
  15.1 43.7 %collective-permute-start.2 = (s32[8,4]{1,0:T(8,128)}, s32[8,4]{1,0:T(8,128)S(1)}, u32[]{:S(2)}, u32[]{:S(2)}) collective-permute-start(s32[8,4]{1,0:T(8,128)} %get-tuple-element.23), channel_id=1, source_target_pairs={{0,1},{1,0},{2,3},{3,2},{4,5},{5,4},{6,7},{7,6},{8,9},{9,8},{10,11... | collective-permute-start | bytes 392 | tf_op jit(solution)/shard_map/ppermute | solution.py:14
  15.5 57.5 %collective-permute-start.4 = (bf16[1,4,8,4,160]{4,3,2,1,0:T(4,128)(2,1)S(1)}, bf16[1,4,8,4,160]{4,3,2,1,0:T(4,128)(2,1)S(1)}, u32[]{:S(2)}, u32[]{:S(2)}) collective-permute-start(bf16[1,4,8,4,160]{4,3,2,1,0:T(4,128)(2,1)S(1)} %get-tuple-element.19), channel_id=1, source_target_pairs={{0,1},{1,0},{2,3},{3,2},{4,5},{5,4},{6,7},{7,6},{8,9},{9,8},{10,11... | collective-permute-start | bytes 122888 | tf_op jit(solution)/shard_map/ppermute | solution.py:14
  56.6 3.9 %copy-start.8 = (f32[5]{0:T(128)S(1)}, f32[5]{0:T(128)}, u32[]{:S(2)}) copy-start(f32[5]{0:T(128)} %param.13) | copy-start | bytes 64
  56.6 16.2 %copy-start.9 = (f32[8]{0:T(128)S(1)}, f32[8]{0:T(128)}, u32[]{:S(2)}) copy-start(f32[8]{0:T(128)} %fusion.27) | copy-start | bytes 100
  58.8 18.8 %collective-permute-start.1 = (bf16[1,4,4,8,4608]{4,3,2,1,0:T(8,128)(2,1)}, bf16[1,4,4,8,4608]{4,3,2,1,0:T(8,128)(2,1)S(1)}, u32[]{:S(2)}, u32[]{:S(2)}) collective-permute-start(bf16[1,4,4,8,4608]{4,3,2,1,0:T(8,128)(2,1)} %get-tuple-element.11), channel_id=1, source_target_pairs={{0,6},{2,0},{4,2},{6,4},{1,7},{3,1},{5,3},{7,5},{8,14},{10,8},{12,... | collective-permute-start | bytes 3538952 | tf_op jit(solution)/shard_map/ppermute | solution.py:14
  58.9 14.0 %collective-permute-start.3 = (s32[4,8]{1,0:T(4,128)S(1)}, s32[4,8]{1,0:T(4,128)S(1)}, u32[]{:S(2)}, u32[]{:S(2)}) collective-permute-start(s32[4,8]{1,0:T(4,128)S(1)} %get-tuple-element.21), channel_id=1, source_target_pairs={{0,6},{2,0},{4,2},{6,4},{1,7},{3,1},{5,3},{7,5},{8,14},{10,8},{12,... | collective-permute-start | bytes 392 | tf_op jit(solution)/shard_map/ppermute | solution.py:14
  73.1 4.4 %collective-permute-start.5 = (bf16[1,4,4,8,160]{4,3,2,1,0:T(8,128)(2,1)S(1)}, bf16[1,4,4,8,160]{4,3,2,1,0:T(8,128)(2,1)S(1)}, u32[]{:S(2)}, u32[]{:S(2)}) collective-permute-start(bf16[1,4,4,8,160]{4,3,2,1,0:T(8,128)(2,1)S(1)} %get-tuple-element.17), channel_id=1, source_target_pairs={{0,6},{2,0},{4,2},{6,4},{1,7},{3,1},{5,3},{7,5},{8,14},{10,8},{12,... | collective-permute-start | bytes 122888 | tf_op jit(solution)/shard_map/ppermute | solution.py:14
  79.2 2.3 %copy-start = (bf16[2,128,1536]{1,2,0:T(8,128)(2,1)S(1)}, bf16[2,128,1536]{1,2,0:T(8,128)(2,1)}, u32[]{:S(2)}) copy-start(bf16[2,128,1536]{1,2,0:T(8,128)(2,1)} %copy.29) | copy-start | bytes 2359300
  79.2 2.3 %copy-start.5 = (pred[128,128]{0,1:T(8,128)(4,1)S(1)}, pred[128,128]{0,1:T(8,128)(4,1)}, u32[]{:S(2)}) copy-start(pred[128,128]{0,1:T(8,128)(4,1)} %broadcast_compare_fusion) | copy-start | bytes 49156
  80.4 1.2 copy-start.1
  81.6 4.2 %copy-start.2 = (bf16[2,128,1536]{1,2,0:T(8,128)(2,1)S(1)}, bf16[2,128,1536]{1,2,0:T(8,128)(2,1)}, u32[]{:S(2)}) copy-start(bf16[2,128,1536]{1,2,0:T(8,128)(2,1)} %copy.28) | copy-start | bytes 2359300
Sparse Core Ops, SparseCore 0:
  9.6 99.9 all-gather.2
  116.8 21.7 reduce-scatter.3
where the time goes:
time: 178 us
  blocking collectives  65.2 us (37%)
  waiting for transfers between devices  50 us (28%)
  matrix products  17.8 us (10%)
  between operations  15.6 us (9%)
  local copies, waits for them, and re-layouts  13.3 us (7%)
  starting transfers between devices  9.26 us (5%)
  other arithmetic  6.65 us (4%)
    psum x1, blocking collectives, shards(): grad_sum, loss_sum = lax.psum((grad_shard, shard_penalty), ('lat', 'lon'))  30.5 us
    all_gather x1, blocking collectives, shards(): lax.all_gather(unpatch_matrix, 'dp', axis=0, tiled=True)  21.7 us
    all_gather x1, waiting for transfers between devices, shards(): lax.all_gather(w_out, 'dp', axis=0, tiled=True)  19.3 us
    unnamed x3, waiting for transfers between devices  16.6 us
    ppermute x6, waiting for transfers between devices, from_behind(): lax.ppermute(array, axis, [(i, (i + by) % length) for i in range(length)])  14.1 us
    all_gather x1, blocking collectives, shards(): lax.all_gather(norm_gain, 'dp', axis=0, tiled=True)  13 us
    ppermute x6, starting transfers between devices, from_behind(): lax.ppermute(array, axis, [(i, (i + by) % length) for i in range(length)])  9.19 us
    dot_general x1, matrix products, shards(): jnp.einsum('tj,ij->ti', grad_mixed, out_all, preferred_element_type=jnp.f...  4.79 us
  transfers between devices with their start and end apart: 8, of which 4 were waited for; matrix products, arithmetic and copies ran while one was open for 16% of the time, Pallas kernels for 0%

commit v1 on v0

--- a/solution.py
+++ b/solution.py
@@ -100,7 +100,7 @@
         scatter_dimension=0,
         tiled=True,
     ).astype(jnp.float32)
-    grad_sum, loss_sum = lax.psum((grad_shard, shard_penalty), ("lat", "lon"))
+    grad_sum, loss_sum = lax.psum(lax.psum((grad_shard, shard_penalty), "lon"), "lat")
     grad_recovery = grad_sum / (levels * lat_total * lon_total)
     grad_hidden = jnp.einsum(
         "to,do->td", prediction_gradient, unprojected_pieces, preferred_element_type=jnp.float32

time: 178 us -> 190 us (1.067)
  waiting for transfers between devices: 50 us -> 70.9 us
  blocking collectives: 65.2 us -> 53.9 us
    psum x0 -> x1, waiting for transfers between devices: none -> 17.1 us  [shards(): lax.psum(lax.psum((grad_shard, shard_penalty), 'lon'), 'lat')]
    psum x1 -> x2, blocking collectives: 30.5 us -> 19.2 us  [the longest x1 12.9 us: shards(): lax.psum((grad_shard, shard_penalty), 'lon')]
    unnamed x3 -> x4, waiting for transfers between devices: 16.6 us -> 20.3 us
  transfers between devices with their start and end apart: 8 -> 9, of which waited for: 4 -> 5; matrix products, arithmetic and copies ran while one was open for 16% -> 16% of each run, Pallas kernels for 0% -> 0%
where the time goes in v1:
time: 190 us; the launch traced here: 189 us
  waiting for transfers between devices  70.9 us (37%)
  blocking collectives  53.9 us (28%)
  matrix products  19.3 us (10%)
  between operations  15.2 us (8%)
  local copies, waits for them, and re-layouts  13.3 us (7%)
  starting transfers between devices  9.13 us (5%)
  other arithmetic  7.58 us (4%)
    all_gather x1, blocking collectives, shards(): lax.all_gather(unpatch_matrix, 'dp', axis=0, tiled=True)  21.7 us
    unnamed x4, waiting for transfers between devices  20.3 us
    all_gather x1, waiting for transfers between devices, shards(): lax.all_gather(w_out, 'dp', axis=0, tiled=True)  19.5 us
    psum x1, waiting for transfers between devices, shards(): lax.psum(lax.psum((grad_shard, shard_penalty), 'lon'), 'lat')  17.1 us
    ppermute x6, waiting for transfers between devices, from_behind(): lax.ppermute(array, axis, [(i, (i + by) % length) for i in range(length)])  14.1 us
    all_gather x1, blocking collectives, shards(): lax.all_gather(norm_gain, 'dp', axis=0, tiled=True)  13 us
    psum x1, blocking collectives, shards(): lax.psum((grad_shard, shard_penalty), 'lon')  12.9 us
    ppermute x6, starting transfers between devices, from_behind(): lax.ppermute(array, axis, [(i, (i + by) % length) for i in range(length)])  9.01 us
  transfers between devices with their start and end apart: 9, of which 5 were waited for; matrix products, arithmetic and copies ran while one was open for 16% of the time, Pallas kernels for 0%

profile of v1, /device:TPU:0, one launch (start us, length us, event | category | flops | bytes accessed | tf_op | source)
XLA Modules:
  0.0 189.3 jit_solution(8232641488196756235)
XLA Ops:
  7.2 0.7 all-gather.3.cloned.1.call-update
  7.9 3.3 %fusion.33 = (bf16[1,4,8,4,4608]{4,3,2,1,0:T(4,128)(2,1)S(1)}, bf16[1,4,8,4,4608]{4,3,2,1,0:T(4,128)(2,1)S(1)}) fusion(bf16[1,4,8,8,4608]{4,3,2,1,0:T(8,128)(2,1)} %param.7), kind=kLoop, calls=%fused_computation.70 | loop fusion | bytes 4718592 | tf_op jit(solution)/shard_map/slice | solution.py:31
  11.5 3.0 %collective-permute-start = (bf16[1,4,8,4,4608]{4,2,3,1,0:T(8,128)(2,1)S(1)}, bf16[1,4,8,4,4608]{4,2,3,1,0:T(8,128)(2,1)}, u32[]{:S(2)}, u32[]{:S(2)}) collective-permute-start(bf16[1,4,8,4,4608]{4,2,3,1,0:T(8,128)(2,1)S(1)} %copy.37), channel_id=1, source_target_pairs={{0,1},{1,0},{2,3},{3,2},{4,5},{5,4},{6,7},{7,6},{8,9},{9,8},{10,11... | collective-permute-start | bytes 3538952 | tf_op jit(solution)/shard_map/ppermute | solution.py:14
  15.5 1.7 collective-permute-start.4
  17.4 13.0 %all-gather = bf16[4,1,384]{2,1,0:T(2,128)(2,1)S(1)} all-gather(bf16[1,1,384]{2,1,0:T(2,128)(2,1)S(1)} %reshape.165), channel_id=1, replica_groups=mesh['dp'=4,'lat'=4,'lon'=2] {'dp'}, dimensions={0}, use_global_device_ids=true | all-gather | bytes 3840 | tf_op jit(solution)/shard_map/all_gather | solution.py:66
  30.4 0.6 cosine_reduce_fusion
  32.3 21.7 %all_gather.11 = bf16[1536,160]{0,1:T(8,128)(2,1)S(1)} all-gather(bf16[384,160]{0,1:T(8,128)(2,1)S(1)} %copy-done.4), channel_id=1, replica_groups=mesh['dp'=4,'lat'=4,'lon'=2] {'dp'}, dimensions={0}, use_global_device_ids=true | all-gather | bytes 614400 | tf_op jit(solution)/shard_map/all_gather | solution.py:65
  54.0 0.7 broadcast_compare_fusion
  54.7 1.9 copy.27
  56.6 2.2 %fusion.8 = (bf16[1,4,4,8,4608]{4,3,2,1,0:T(8,128)(2,1)S(1)}, bf16[1,4,4,8,4608]{4,3,2,1,0:T(8,128)(2,1)}) fusion(bf16[1,4,8,4,4608]{4,3,2,1,0:T(4,128)(2,1)S(1)} %get-tuple-element.12, bf16[1,4,8,4,4608]{4,3,2,1,0:T(4,128)(2,1)S(1)} %copy.27), kind=kLoop, calls=%fused_computation.22 | loop fusion | flops 4718592 | bytes 4718592 | tf_op jit(solution)/shard_map/concatenate | solution.py:31
  58.8 1.6 collective-permute-start.3
  60.6 12.2 %collective-permute-done.3 = s32[4,8]{1,0:T(4,128)S(1)} collective-permute-done((s32[4,8]{1,0:T(4,128)S(1)}, s32[4,8]{1,0:T(4,128)S(1)}, u32[]{:S(2)}, u32[]{:S(2)}) %collective-permute-start.3) | collective-permute-done | bytes 160 | tf_op jit(solution)/shard_map/ppermute | solution.py:14
  73.1 2.3 %collective-permute-start.5 = (bf16[1,4,4,8,160]{4,3,2,1,0:T(8,128)(2,1)S(1)}, bf16[1,4,4,8,160]{4,3,2,1,0:T(8,128)(2,1)S(1)}, u32[]{:S(2)}, u32[]{:S(2)}) collective-permute-start(bf16[1,4,4,8,160]{4,3,2,1,0:T(8,128)(2,1)S(1)} %get-tuple-element.17), channel_id=1, source_target_pairs={{0,6},{2,0},{4,2},{6,4},{1,7},{3,1},{5,3},{7,5},{8,14},{10,8},{12,... | collective-permute-start | bytes 122888 | tf_op jit(solution)/shard_map/ppermute | solution.py:14
  75.3 1.9 %collective-permute-done.5 = bf16[1,4,4,8,160]{4,3,2,1,0:T(8,128)(2,1)S(1)} collective-permute-done((bf16[1,4,4,8,160]{4,3,2,1,0:T(8,128)(2,1)S(1)}, bf16[1,4,4,8,160]{4,3,2,1,0:T(8,128)(2,1)S(1)}, u32[]{:S(2)}, u32[]{:S(2)}) %collective-permute-start.5) | collective-permute-done | bytes 40992 | tf_op jit(solution)/shard_map/ppermute | solution.py:14
  77.9 1.2 copy.29
  79.0 1.2 copy.30
  80.2 1.2 copy.28
  81.4 4.2 %fusion.37 = (f32[2,48,128]{2,1,0:T(8,128)S(1)}, f32[2,48,128,128]{2,3,1,0:T(8,128)}) fusion(pred[128,128]{0,1:T(8,128)(4,1)S(1)} %copy-done.5, bf16[2,128,48,32]{1,3,2,0:T(8,128)(2,1)S(1)} %bitcast.35, bf16[2,128,48,32]{1,3,2,0:T(8,128)(2,1)S(1)} %bitcast.36), kind=kOutput, calls=%fused_computation.74 | convolution fusion | flops 106954880 | bytes 7929856 | tf_op jit(solution)/shard_map/sub | solution.py:58
  85.6 3.7 %fusion.7 = bf16[2,128,48,32]{1,3,2,0:T(8,128)(2,1)S(1)} fusion(bf16[2,128,48,32]{1,3,2,0:T(8,128)(2,1)S(1)} %bitcast.37, f32[2,48,128,128]{2,3,1,0:T(8,128)} %get-tuple-element.25, f32[2,48,128]{2,1,0:T(8,128)S(1)} %get-tuple-element.24), kind=kOutput, calls=%fused_computation.21 | convolution fusion | flops 104202240 | bytes 7913472 | tf_op jit(solution)/shard_map/whqk,wkhd->wqhd/dot_general | solution.py:60
  89.3 0.8 copy.32
  90.1 19.5 %all-gather.3.cloned.1.call-done = bf16[1536,1536]{1,0:T(8,128)(2,1)} async-done(((bf16[384,1536]{1,0:T(8,128)(2,1)}), bf16[1536,1536]{1,0:T(8,128)(2,1)}) %all-gather.3.cloned.1.call-update) | async-done | bytes 4718608 | tf_op jit(solution)/shard_map/all_gather | solution.py:64
  109.6 3.8 %fusion.38 = (f32[256]{0:T(256)S(1)}, f32[256,1536]{1,0:T(8,128)S(1)}) fusion(bf16[1536,1536]{1,0:T(8,128)(2,1)} %all-gather.3.cloned.1.call-done, bf16[192,8,2,128]{3,2,1,0:T(2,128)(2,1)S(1)} %bitcast.38), kind=kOutput, calls=%fused_computation.75 | convolution fusion | flops 1208352512 | bytes 7078912 | tf_op jit(solution)/shard_map/dot_general | solution.py:68
  114.4 0.7 fusion.18
  115.5 1.2 copy.35
  117.3 1.7 fusion.31
  119.0 19.6 %reduce-scatter.4.cloned.1.call-done = bf16[384,160]{1,0:T(8,128)(2,1)} async-done(((bf16[1536,160]{1,0:T(8,128)(2,1)}), bf16[384,160]{1,0:T(8,128)(2,1)}) %reduce-scatter.4.cloned.1.call-update) | async-done | bytes 122896
  138.6 1.1 copy.36
  139.6 12.9 %all-reduce.5 = (f32[384,160]{0,1:T(8,128)}, f32[]{:T(128)}) all-reduce(bf16[384,160]{0,1:T(8,128)(2,1)S(1)} %copy.36, f32[]{:T(128)S(6)} %div.65), channel_id=1, replica_groups=mesh['dp'=4,'lat'=4,'lon'=2] {'lon'}, use_global_device_ids=true, to_apply=%region_8.9 | all-reduce | flops 61441 | bytes 368648 | tf_op jit(solution)/shard_map/psum | solution.py:103
  152.6 5.2 %convolution_convert_fusion = bf16[256,1536]{1,0:T(8,128)(2,1)} fusion(bf16[1536,1536]{1,0:T(8,128)(2,1)} %all-gather.3.cloned.1.call-done, f32[256,1536]{1,0:T(8,128)} %get-tuple-element.28, f32[256,1536]{1,0:T(8,128)S(1)} %get-tuple-element.27, f32[256]{0:T(256)S(1)} %get-tuple-element.29, f32[256]{0:T(256)S(1)} %get-tuple-element.30, ...), kind=kOutput, calls=%fused_computation.10 | convolution fusion | flops 1211105280 | bytes 8654848 | tf_op jit(solution)/shard_map/tj,ij->ti/dot_general | solution.py:115
  157.8 6.3 %psum.31 = f32[1]{0:T(128)} all-reduce(f32[1]{0:T(128)} %bitcast.7), channel_id=1, replica_groups=mesh['dp'=4,'lat'=4,'lon'=2] {'lat'}, use_global_device_ids=true, to_apply=%region_12.13 | all-reduce | flops 1 | bytes 8 | tf_op jit(solution)/shard_map/psum | solution.py:103
  164.1 17.1 %all-reduce.4.cloned.1.call-done = f32[384,160]{0,1:T(8,128)} async-done(((f32[384,160]{0,1:T(8,128)}), f32[384,160]{0,1:T(8,128)}) %all-reduce.4.cloned.1.call-update) | async-done | bytes 245776 | tf_op jit(solution)/shard_map/psum | solution.py:103
  181.2 1.7 broadcast_multiply_fusion
  (62 shorter events, 4.6 us)
Async XLA Ops:
  7.2 102.4 %all-gather.3.cloned.1.call-start = ((), (), s32[]{:S(2)}) async-start(), calls=%async_computation.1 | async-start | bytes 5898240 | tf_op jit(solution)/shard_map/all_gather | solution.py:64
  7.9 130.7 %reduce-scatter.4.cloned.1.call-start = ((), (), s32[]{:S(2)}) async-start(), calls=%async_computation.3 | async-start | bytes 983040
  11.2 3.3 %copy-start.6 = (s32[8,8]{1,0:T(8,128)S(1)}, s32[8,8]{1,0:T(8,128)}, u32[]{:S(2)}) copy-start(s32[8,8]{1,0:T(8,128)} %param.9) | copy-start | bytes 772
  11.2 4.2 %copy-start.3 = (bf16[1,4,8,8,160]{4,3,2,1,0:T(8,128)(2,1)S(1)}, bf16[1,4,8,8,160]{4,3,2,1,0:T(8,128)(2,1)}, u32[]{:S(2)}) copy-start(bf16[1,4,8,8,160]{4,3,2,1,0:T(8,128)(2,1)} %param.8) | copy-start | bytes 245764
  11.3 6.1 %copy-start.7 = (bf16[384]{0:T(512)(128)(2,1)S(1)}, bf16[384]{0:T(512)(128)(2,1)}, u32[]{:S(2)}) copy-start(bf16[384]{0:T(512)(128)(2,1)} %param.12) | copy-start | bytes 2308
  11.3 21.0 %copy-start.4 = (bf16[384,160]{0,1:T(8,128)(2,1)S(1)}, bf16[384,160]{0,1:T(8,128)(2,1)}, u32[]{:S(2)}) copy-start(bf16[384,160]{0,1:T(8,128)(2,1)} %param.11) | copy-start | bytes 368644
  11.5 43.2 %collective-permute-start = (bf16[1,4,8,4,4608]{4,2,3,1,0:T(8,128)(2,1)S(1)}, bf16[1,4,8,4,4608]{4,2,3,1,0:T(8,128)(2,1)}, u32[]{:S(2)}, u32[]{:S(2)}) collective-permute-start(bf16[1,4,8,4,4608]{4,2,3,1,0:T(8,128)(2,1)S(1)} %copy.37), channel_id=1, source_target_pairs={{0,1},{1,0},{2,3},{3,2},{4,5},{5,4},{6,7},{7,6},{8,9},{9,8},{10,11... | collective-permute-start | bytes 3538952 | tf_op jit(solution)/shard_map/ppermute | solution.py:14
  15.1 43.7 %collective-permute-start.2 = (s32[8,4]{1,0:T(8,128)}, s32[8,4]{1,0:T(8,128)S(1)}, u32[]{:S(2)}, u32[]{:S(2)}) collective-permute-start(s32[8,4]{1,0:T(8,128)} %get-tuple-element.23), channel_id=1, source_target_pairs={{0,1},{1,0},{2,3},{3,2},{4,5},{5,4},{6,7},{7,6},{8,9},{9,8},{10,11... | collective-permute-start | bytes 392 | tf_op jit(solution)/shard_map/ppermute | solution.py:14
  15.5 57.5 %collective-permute-start.4 = (bf16[1,4,8,4,160]{4,3,2,1,0:T(4,128)(2,1)S(1)}, bf16[1,4,8,4,160]{4,3,2,1,0:T(4,128)(2,1)S(1)}, u32[]{:S(2)}, u32[]{:S(2)}) collective-permute-start(bf16[1,4,8,4,160]{4,3,2,1,0:T(4,128)(2,1)S(1)} %get-tuple-element.19), channel_id=1, source_target_pairs={{0,1},{1,0},{2,3},{3,2},{4,5},{5,4},{6,7},{7,6},{8,9},{9,8},{10,11... | collective-permute-start | bytes 122888 | tf_op jit(solution)/shard_map/ppermute | solution.py:14
  56.6 3.9 %copy-start.8 = (f32[5]{0:T(128)S(1)}, f32[5]{0:T(128)}, u32[]{:S(2)}) copy-start(f32[5]{0:T(128)} %param.13) | copy-start | bytes 64
  56.6 16.2 %copy-start.9 = (f32[8]{0:T(128)S(1)}, f32[8]{0:T(128)}, u32[]{:S(2)}) copy-start(f32[8]{0:T(128)} %fusion.27) | copy-start | bytes 100
  58.8 18.7 %collective-permute-start.1 = (bf16[1,4,4,8,4608]{4,3,2,1,0:T(8,128)(2,1)}, bf16[1,4,4,8,4608]{4,3,2,1,0:T(8,128)(2,1)S(1)}, u32[]{:S(2)}, u32[]{:S(2)}) collective-permute-start(bf16[1,4,4,8,4608]{4,3,2,1,0:T(8,128)(2,1)} %get-tuple-element.11), channel_id=1, source_target_pairs={{0,6},{2,0},{4,2},{6,4},{1,7},{3,1},{5,3},{7,5},{8,14},{10,8},{12,... | collective-permute-start | bytes 3538952 | tf_op jit(solution)/shard_map/ppermute | solution.py:14
  58.8 14.0 %collective-permute-start.3 = (s32[4,8]{1,0:T(4,128)S(1)}, s32[4,8]{1,0:T(4,128)S(1)}, u32[]{:S(2)}, u32[]{:S(2)}) collective-permute-start(s32[4,8]{1,0:T(4,128)S(1)} %get-tuple-element.21), channel_id=1, source_target_pairs={{0,6},{2,0},{4,2},{6,4},{1,7},{3,1},{5,3},{7,5},{8,14},{10,8},{12,... | collective-permute-start | bytes 392 | tf_op jit(solution)/shard_map/ppermute | solution.py:14
  73.1 4.2 %collective-permute-start.5 = (bf16[1,4,4,8,160]{4,3,2,1,0:T(8,128)(2,1)S(1)}, bf16[1,4,4,8,160]{4,3,2,1,0:T(8,128)(2,1)S(1)}, u32[]{:S(2)}, u32[]{:S(2)}) collective-permute-start(bf16[1,4,4,8,160]{4,3,2,1,0:T(8,128)(2,1)S(1)} %get-tuple-element.17), channel_id=1, source_target_pairs={{0,6},{2,0},{4,2},{6,4},{1,7},{3,1},{5,3},{7,5},{8,14},{10,8},{12,... | collective-permute-start | bytes 122888 | tf_op jit(solution)/shard_map/ppermute | solution.py:14
  79.0 2.3 %copy-start = (bf16[2,128,1536]{1,2,0:T(8,128)(2,1)S(1)}, bf16[2,128,1536]{1,2,0:T(8,128)(2,1)}, u32[]{:S(2)}) copy-start(bf16[2,128,1536]{1,2,0:T(8,128)(2,1)} %copy.29) | copy-start | bytes 2359300
  79.0 2.3 %copy-start.5 = (pred[128,128]{0,1:T(8,128)(4,1)S(1)}, pred[128,128]{0,1:T(8,128)(4,1)}, u32[]{:S(2)}) copy-start(pred[128,128]{0,1:T(8,128)(4,1)} %broadcast_compare_fusion) | copy-start | bytes 49156
  80.2 1.2 copy-start.1
  81.4 4.2 %copy-start.2 = (bf16[2,128,1536]{1,2,0:T(8,128)(2,1)S(1)}, bf16[2,128,1536]{1,2,0:T(8,128)(2,1)}, u32[]{:S(2)}) copy-start(bf16[2,128,1536]{1,2,0:T(8,128)(2,1)} %copy.28) | copy-start | bytes 2359300
  116.6 64.5 %all-reduce.4.cloned.1.call-start = ((), (), s32[]{:S(2)}) async-start(), calls=%async_computation.2 | async-start | bytes 491520 | tf_op jit(solution)/shard_map/psum | solution.py:103
Sparse Core Ops, SparseCore 0:
  9.6 99.9 all-gather.2
  116.8 21.7 reduce-scatter.3
  152.7 28.4 all-reduce.3
